TPU v7x, 32 devices: a whole 2x2x4 slice. The times are simulated.
32 devices in a mesh: blk: 8 (over z, core), grp: 4 (over y, x).
Axes of the slice: x: 2, y: 2, z: 4, core: 2. Of those that a mesh axis runs over, the one named last changes fastest.
Arguments:
- state: float32 [4, 5, 128, 256], P('grp', None, 'blk'), may hold values from -6 to 6
- advection: float32 [4, 2, 128, 256], P('grp', None, 'blk'), may hold values from 0.2 to 1
- viscosity: float32 [4, 2, 128, 256], P('grp', None, 'blk'), may hold values from 0.01 to 0.2
- donor_cell: int32 [8, 4, 4, 32], P('blk', 'grp'), may hold values from 0 to 3839
- donor_frac: float32 [8, 4, 2, 4, 32], P('blk', 'grp'), may hold values from 0 to 1
- fringe_cell: int32 [8, 4, 4, 32], P('blk', 'grp'), may hold values from 768 to 3327, as said below
- fringe_count: int32 [8, 4, 4], P('blk', 'grp'), may hold values from 1 to 32, as said below
Outputs:
- final_state: float32 [4, 5, 128, 256], P('grp', None, 'blk')
Inputs may be any that keep to these rules, and one draw needn't show every extreme that they name: `fringe_cell`: for each receiving block, all entries over source groups and slots are distinct, and every one lies in rows 3 to 12 of the block. `fringe_count`: for every receiving block, one source group has exactly 32 live slots.
All inputs are finite; a program needn't handle non-finite values.
Results may differ from a plain program's by a relative error of at most 0.00005.
Values sent between devices are 32-bit elements; how exact they have to be, the bound alone decides.
A program may use at most 64 MiB of HBM per device.

v0:
```python
import jax
import jax.numpy as jnp
from jax import lax
from jax.sharding import PartitionSpec as P

STEPS = 2


TIME_STEP = 0.3
SECTION_COEFS = ((0.0, 1.0), (0.75, 0.25), (1.0 / 3.0, 2.0 / 3.0))


def with_halo(x, sides, width):
    for axis, dim in sides:
        count, length = (lax.axis_size(axis), x.shape[dim])
        up = [(i, (i + 1) % count) for i in range(count - 1)]
        down = [(j, i) for i, j in up]
        last = lax.slice_in_dim(x, length - width, length, axis=dim)
        first = lax.slice_in_dim(x, 0, width, axis=dim)
        before = lax.ppermute(last, axis, up)
        after = lax.ppermute(first, axis, down)
        x = jnp.concatenate([before, x, after], axis=dim)
    return x


def tendency(padded, speed_x, speed_y, visc_x, visc_y):
    rows_n = padded.shape[-2] - 6
    row_axis = padded.ndim - 2

    def along_x(offset):
        return lax.slice_in_dim(padded, 3 + offset, 3 + offset + rows_n, axis=row_axis)

    centre = along_x(0)

    def along_y(offset):
        return jnp.roll(centre, -offset, axis=-1)

    upwind_x = (
        -2.0 * along_x(-3)
        + 15.0 * along_x(-2)
        - 60.0 * along_x(-1)
        + 20.0 * centre
        + 30.0 * along_x(1)
        - 3.0 * along_x(2)
    ) / 60.0
    upwind_y = (
        -2.0 * along_y(-3)
        + 15.0 * along_y(-2)
        - 60.0 * along_y(-1)
        + 20.0 * centre
        + 30.0 * along_y(1)
        - 3.0 * along_y(2)
    ) / 60.0
    central_x = (along_x(-2) - 8.0 * along_x(-1) + 8.0 * along_x(1) - along_x(2)) / 12.0
    central_y = (along_y(-2) - 8.0 * along_y(-1) + 8.0 * along_y(1) - along_y(2)) / 12.0
    second_x = along_x(1) - 2.0 * centre + along_x(-1)
    second_y = along_y(1) - 2.0 * centre + along_y(-1)
    transport = -(speed_x * upwind_x + speed_y * upwind_y) + visc_x * second_x + visc_y * second_y
    diverge = central_x[..., 1, :, :] + central_y[..., 2, :, :]
    grad_x = central_x[..., 4, :, :]
    grad_y = central_y[..., 4, :, :]
    acoustic = jnp.stack([-diverge, -grad_x, -grad_y, jnp.zeros_like(diverge), -diverge], axis=-3)
    return transport + acoustic


def block_faces(field):
    return with_halo(field, (("blk", 1),), 3)


def one_hot(index, width):
    return (index[..., None] == jnp.arange(width, dtype=jnp.int32)).astype(jnp.float32)


def fringe_local(field, corner, frac_x, frac_y, target_cell, live_count):
    nvar, rows_n, cols_n = field.shape
    groups_n, slots = corner.shape

    def interpolate(inputs):
        corner_row, weight_x, weight_y = inputs
        row_index = corner_row // cols_n
        col_index = corner_row % cols_n
        row_weight = (1.0 - weight_x)[:, None] * one_hot(row_index, rows_n) + weight_x[
            :, None
        ] * one_hot(row_index + 1, rows_n)
        col_weight = (1.0 - weight_y)[:, None] * one_hot(col_index, cols_n) + weight_y[
            :, None
        ] * one_hot((col_index + 1) % cols_n, cols_n)
        partial_rows = jnp.einsum("kr,vrc->vkc", row_weight, field, precision=lax.Precision.HIGHEST)
        return jnp.sum(partial_rows * col_weight[None], axis=-1)

    values = lax.map(interpolate, (corner, frac_x, frac_y))
    outgoing = values.reshape(groups_n, nvar * slots)
    incoming = lax.all_to_all(outgoing, "grp", split_axis=0, concat_axis=0, tiled=True)
    incoming = (
        incoming.reshape(groups_n, nvar, slots).transpose(1, 0, 2).reshape(nvar, groups_n * slots)
    )
    live = (
        (jnp.arange(slots, dtype=jnp.int32)[None, :] < live_count[:, None])
        .astype(jnp.float32)
        .reshape(-1)
    )
    target = target_cell.reshape(-1)
    target_rows = one_hot(target // cols_n, rows_n) * live[:, None]
    target_cols = one_hot(target % cols_n, cols_n)
    placed = jnp.einsum(
        "vkr,kc->vrc",
        incoming[:, :, None] * target_rows[None],
        target_cols,
        precision=lax.Precision.HIGHEST,
    )
    hit_count = jnp.einsum("kr,kc->rc", target_rows, target_cols, precision=lax.Precision.HIGHEST)
    return jnp.where(hit_count[None] > 0.5, placed, field)


def body(state, advection, viscosity, donor_cell, donor_frac, fringe_cell, fringe_count):
    start = state[0]
    speed_x = advection[0, 0:1]
    speed_y = advection[0, 1:2]
    visc_x = viscosity[0, 0:1]
    visc_y = viscosity[0, 1:2]
    corner = donor_cell[0, 0]
    frac_x = donor_frac[0, 0, 0]
    frac_y = donor_frac[0, 0, 1]
    target_cell = fringe_cell[0, 0]
    live_count = fringe_count[0, 0]
    for step_index in range(STEPS):
        section_field = start
        for weight_old, weight_new in SECTION_COEFS:
            raw_padded = block_faces(section_field)
            filled = fringe_local(section_field, corner, frac_x, frac_y, target_cell, live_count)
            padded = jnp.concatenate([raw_padded[:, :3], filled, raw_padded[:, -3:]], axis=1)
            result = filled + TIME_STEP * tendency(padded, speed_x, speed_y, visc_x, visc_y)
            section_field = weight_old * start + weight_new * result
        start = section_field
    return start[None]


def solution(mesh):
    placed = (
        P("grp", None, "blk", None),
        P("grp", None, "blk", None),
        P("grp", None, "blk", None),
        P("blk", "grp", None, None),
        P("blk", "grp", None, None, None),
        P("blk", "grp", None, None),
        P("blk", "grp", None),
    )
    return jax.shard_map(
        body, mesh=mesh, in_specs=placed, out_specs=P("grp", None, "blk", None), check_vma=False
    )
```

profile of v0, /device:TPU:1, one launch (start us, length us, event | category | flops | bytes accessed | tf_op | source)
XLA Modules:
  0.0 97.8 jit_solution(14620769271471472965)
XLA Ops:
  0.0 0.7 slice_bitcast_fusion.2
  0.7 0.7 copy-done.1
  1.4 5.9 %while.72 = (s32[]{:T(128)}, f32[4,5,32]{2,1,0:T(8,128)S(1)}, s32[4,32]{1,0:T(4,128)S(1)}, f32[4,32]{1,0:T(4,128)S(1)}, f32[5,16,256]{2,1,0:T(8,128)}, /*index=5*/f32[4,32]{1,0:T(4,128)S(1)}, s32[]{:T(128)}) while((s32[]{:T(128)}, f32[4,5,32]{2,1,0:T(8,128)S(1)}, s32[4,32]{1,0:T(4,128)S(1)}, f32[4,32]{1,0:T(4,128)S(1)}, ...), condition=%wide.region_2.3_spmd, body=%wide.region_0.2_spmd.sunk | while | flops 7990722 | bytes 159065 | solution.py:91
  1.5 1.3 %fusion.340 = f32[32,5]{0,1:T(8,128)S(1)} fusion(f32[5,16,256]{2,1,0:T(8,128)} %get-tuple-element.1047, f32[32,256]{1,0:T(8,128)S(1)} %select_add_fusion.12, f32[32]{0:T(128)S(1)} %get-tuple-element.950, s32[32]{0:T(128)S(1)} %get-tuple-element.951, f32[32]{0:T(128)S(1)} %get-tuple-element.952, s32[32]{0:T(128)S(1)} %get-tuple-element.953), kind=kOutput, calls=%fused_computation.1.clone.1 | convolution fusion | flops 7948640 | bytes 115840 | tf_op jit(solution)/shard_map/while/body/eval_jaxpr/kr,vrc->vkc/dot_general | solution.py:88
  3.0 1.3 %fusion.340 = f32[32,5]{0,1:T(8,128)S(1)} fusion(f32[5,16,256]{2,1,0:T(8,128)} %get-tuple-element.1047, f32[32,256]{1,0:T(8,128)S(1)} %select_add_fusion.12, f32[32]{0:T(128)S(1)} %get-tuple-element.950, s32[32]{0:T(128)S(1)} %get-tuple-element.951, f32[32]{0:T(128)S(1)} %get-tuple-element.952, s32[32]{0:T(128)S(1)} %get-tuple-element.953), kind=kOutput, calls=%fused_computation.1.clone.1 | convolution fusion | flops 7948640 | bytes 115840 | tf_op jit(solution)/shard_map/while/body/eval_jaxpr/kr,vrc->vkc/dot_general | solution.py:88
  4.5 1.3 %fusion.340 = f32[32,5]{0,1:T(8,128)S(1)} fusion(f32[5,16,256]{2,1,0:T(8,128)} %get-tuple-element.1047, f32[32,256]{1,0:T(8,128)S(1)} %select_add_fusion.12, f32[32]{0:T(128)S(1)} %get-tuple-element.950, s32[32]{0:T(128)S(1)} %get-tuple-element.951, f32[32]{0:T(128)S(1)} %get-tuple-element.952, s32[32]{0:T(128)S(1)} %get-tuple-element.953), kind=kOutput, calls=%fused_computation.1.clone.1 | convolution fusion | flops 7948640 | bytes 115840 | tf_op jit(solution)/shard_map/while/body/eval_jaxpr/kr,vrc->vkc/dot_general | solution.py:88
  6.0 1.3 %fusion.340 = f32[32,5]{0,1:T(8,128)S(1)} fusion(f32[5,16,256]{2,1,0:T(8,128)} %get-tuple-element.1047, f32[32,256]{1,0:T(8,128)S(1)} %select_add_fusion.12, f32[32]{0:T(128)S(1)} %get-tuple-element.950, s32[32]{0:T(128)S(1)} %get-tuple-element.951, f32[32]{0:T(128)S(1)} %get-tuple-element.952, s32[32]{0:T(128)S(1)} %get-tuple-element.953), kind=kOutput, calls=%fused_computation.1.clone.1 | convolution fusion | flops 7948640 | bytes 115840 | tf_op jit(solution)/shard_map/while/body/eval_jaxpr/kr,vrc->vkc/dot_general | solution.py:88
  7.3 0.7 all_to_all.48
  8.0 4.2 %all-to-all-start = ((f32[4,1,160]{2,1,0:T(1,128)}), f32[4,1,160]{2,1,0:T(1,128)S(1)}, u32[]{:S(2)}, u32[]{:S(2)}) async-start(f32[4,1,160]{2,1,0:T(1,128)} %all_to_all.48), calls=%async_computation | async-start | bytes 8192 | tf_op jit(solution)/shard_map/all_to_all | solution.py:93
  12.2 0.8 fusion.309
  13.0 4.0 %collective-permute-start = (f32[5,3,256]{2,1,0:T(4,128)S(1)}, f32[5,3,256]{2,1,0:T(4,128)S(1)}, u32[]{:S(2)}, u32[]{:S(2)}) collective-permute-start(f32[5,3,256]{2,1,0:T(4,128)S(1)} %get-tuple-element.680), channel_id=1, source_target_pairs={{0,4},{4,8},{8,12},{12,16},{16,20},{20,24},{24,28},{1,5},{5,9},{9,... | collective-permute-start | bytes 46088 | tf_op jit(solution)/shard_map/ppermute | solution.py:20
  17.1 1.9 %collective-permute-start.1 = (f32[5,3,256]{2,1,0:T(4,128)S(1)}, f32[5,3,256]{2,1,0:T(4,128)S(1)}, u32[]{:S(2)}, u32[]{:S(2)}) collective-permute-start(f32[5,3,256]{2,1,0:T(4,128)S(1)} %get-tuple-element.679), channel_id=1, source_target_pairs={{4,0},{8,4},{12,8},{16,12},{20,16},{24,20},{28,24},{5,1},{9,5},{13... | collective-permute-start | bytes 46088 | tf_op jit(solution)/shard_map/ppermute | solution.py:21
  19.1 0.6 copy-done.5
  20.4 0.4 copy-done
  21.7 0.5 collective-permute-done.1
  22.6 2.4 %while.73 = (s32[]{:T(128)}, f32[4,5,32]{2,1,0:T(8,128)S(1)}, s32[4,32]{1,0:T(4,128)S(1)}, f32[4,32]{1,0:T(4,128)S(1)}, f32[5,16,256]{2,1,0:T(8,128)S(1)}, /*index=5*/f32[4,32]{1,0:T(4,128)S(1)}, s32[]{:T(128)}) while((s32[]{:T(128)}, f32[4,5,32]{2,1,0:T(8,128)S(1)}, s32[4,32]{1,0:T(4,128)S(1)}, f32[4,32]{1,0:T(4,128)S(1)}, ...), condition=%wide.region_5.6_spmd, body=%wide.region_3.5_spmd.sunk | while | flops 7990722 | bytes 159065 | solution.py:91
  22.7 0.4 fusion.343
  23.3 0.4 fusion.343
  23.9 0.4 fusion.343
  24.5 0.4 fusion.343
  25.0 0.7 all_to_all.49
  25.6 3.9 %all-to-all-start.1 = ((f32[4,1,160]{2,1,0:T(1,128)}), f32[4,1,160]{2,1,0:T(1,128)S(1)}, u32[]{:S(2)}, u32[]{:S(2)}) async-start(f32[4,1,160]{2,1,0:T(1,128)} %all_to_all.49), calls=%async_computation.1 | async-start | bytes 8192 | tf_op jit(solution)/shard_map/all_to_all | solution.py:93
  29.6 3.4 %collective-permute-start.2 = (f32[5,3,256]{2,1,0:T(4,128)S(1)}, f32[5,3,256]{2,1,0:T(4,128)S(1)}, u32[]{:S(2)}, u32[]{:S(2)}) collective-permute-start(f32[5,3,256]{2,1,0:T(4,128)S(1)} %get-tuple-element.670), channel_id=1, source_target_pairs={{0,4},{4,8},{8,12},{12,16},{16,20},{20,24},{24,28},{1,5},{5,9},{9,... | collective-permute-start | bytes 46088 | tf_op jit(solution)/shard_map/ppermute | solution.py:20
  33.0 1.9 %collective-permute-start.3 = (f32[5,3,256]{2,1,0:T(4,128)S(1)}, f32[5,3,256]{2,1,0:T(4,128)S(1)}, u32[]{:S(2)}, u32[]{:S(2)}) collective-permute-start(f32[5,3,256]{2,1,0:T(4,128)S(1)} %get-tuple-element.669), channel_id=1, source_target_pairs={{4,0},{8,4},{12,8},{16,12},{20,16},{24,20},{28,24},{5,1},{9,5},{13... | collective-permute-start | bytes 46088 | tf_op jit(solution)/shard_map/ppermute | solution.py:21
  35.9 2.1 %collective-permute-done.3 = f32[5,3,256]{2,1,0:T(4,128)S(1)} collective-permute-done((f32[5,3,256]{2,1,0:T(4,128)S(1)}, f32[5,3,256]{2,1,0:T(4,128)S(1)}, u32[]{:S(2)}, u32[]{:S(2)}) %collective-permute-start.3) | collective-permute-done | bytes 15392 | tf_op jit(solution)/shard_map/ppermute | solution.py:21
  38.4 2.4 %while.74 = (s32[]{:T(128)}, f32[4,5,32]{2,1,0:T(8,128)S(1)}, s32[4,32]{1,0:T(4,128)S(1)}, f32[4,32]{1,0:T(4,128)S(1)}, f32[5,16,256]{2,1,0:T(8,128)S(1)}, /*index=5*/f32[4,32]{1,0:T(4,128)S(1)}, s32[]{:T(128)}) while((s32[]{:T(128)}, f32[4,5,32]{2,1,0:T(8,128)S(1)}, s32[4,32]{1,0:T(4,128)S(1)}, f32[4,32]{1,0:T(4,128)S(1)}, ...), condition=%wide.region_8.9_spmd, body=%wide.region_6.8_spmd.sunk | while | flops 7990722 | bytes 159065 | solution.py:91
  38.6 0.4 fusion.346
  39.2 0.4 fusion.346
  39.8 0.4 fusion.346
  40.4 0.4 fusion.346
  40.8 0.7 all_to_all.50
  41.5 3.9 %all-to-all-start.2 = ((f32[4,1,160]{2,1,0:T(1,128)}), f32[4,1,160]{2,1,0:T(1,128)S(1)}, u32[]{:S(2)}, u32[]{:S(2)}) async-start(f32[4,1,160]{2,1,0:T(1,128)} %all_to_all.50), calls=%async_computation.2 | async-start | bytes 8192 | tf_op jit(solution)/shard_map/all_to_all | solution.py:93
  45.4 2.2 %collective-permute-start.4 = (f32[5,3,256]{2,1,0:T(4,128)S(1)}, f32[5,3,256]{2,1,0:T(4,128)S(1)}, u32[]{:S(2)}, u32[]{:S(2)}) collective-permute-start(f32[5,3,256]{2,1,0:T(4,128)S(1)} %get-tuple-element.660), channel_id=1, source_target_pairs={{0,4},{4,8},{8,12},{12,16},{16,20},{20,24},{24,28},{1,5},{5,9},{9,... | collective-permute-start | bytes 46088 | tf_op jit(solution)/shard_map/ppermute | solution.py:20
  47.7 2.1 %collective-permute-start.5 = (f32[5,3,256]{2,1,0:T(4,128)S(1)}, f32[5,3,256]{2,1,0:T(4,128)S(1)}, u32[]{:S(2)}, u32[]{:S(2)}) collective-permute-start(f32[5,3,256]{2,1,0:T(4,128)S(1)} %get-tuple-element.659), channel_id=1, source_target_pairs={{4,0},{8,4},{12,8},{16,12},{20,16},{24,20},{28,24},{5,1},{9,5},{13... | collective-permute-start | bytes 46088 | tf_op jit(solution)/shard_map/ppermute | solution.py:21
  50.8 2.0 %collective-permute-done.5 = f32[5,3,256]{2,1,0:T(4,128)S(1)} collective-permute-done((f32[5,3,256]{2,1,0:T(4,128)S(1)}, f32[5,3,256]{2,1,0:T(4,128)S(1)}, u32[]{:S(2)}, u32[]{:S(2)}) %collective-permute-start.5) | collective-permute-done | bytes 15392 | tf_op jit(solution)/shard_map/ppermute | solution.py:21
  53.1 2.4 %while.75 = (s32[]{:T(128)}, f32[4,5,32]{2,1,0:T(8,128)S(1)}, s32[4,32]{1,0:T(4,128)S(1)}, f32[4,32]{1,0:T(4,128)S(1)}, f32[5,16,256]{2,1,0:T(8,128)S(1)}, /*index=5*/f32[4,32]{1,0:T(4,128)S(1)}, s32[]{:T(128)}) while((s32[]{:T(128)}, f32[4,5,32]{2,1,0:T(8,128)S(1)}, s32[4,32]{1,0:T(4,128)S(1)}, f32[4,32]{1,0:T(4,128)S(1)}, ...), condition=%wide.region_11.12_spmd, body=%wide.region_9.11_spmd.sunk | while | flops 7990722 | bytes 159065 | solution.py:91
  53.3 0.4 fusion.349
  53.9 0.4 fusion.349
  54.5 0.4 fusion.349
  55.1 0.4 fusion.349
  55.5 0.7 all_to_all.51
  56.2 3.9 %all-to-all-start.3 = ((f32[4,1,160]{2,1,0:T(1,128)}), f32[4,1,160]{2,1,0:T(1,128)S(1)}, u32[]{:S(2)}, u32[]{:S(2)}) async-start(f32[4,1,160]{2,1,0:T(1,128)} %all_to_all.51), calls=%async_computation.3 | async-start | bytes 8192 | tf_op jit(solution)/shard_map/all_to_all | solution.py:93
  60.1 2.2 %collective-permute-start.6 = (f32[5,3,256]{2,1,0:T(4,128)S(1)}, f32[5,3,256]{2,1,0:T(4,128)S(1)}, u32[]{:S(2)}, u32[]{:S(2)}) collective-permute-start(f32[5,3,256]{2,1,0:T(4,128)S(1)} %get-tuple-element.650), channel_id=1, source_target_pairs={{0,4},{4,8},{8,12},{12,16},{16,20},{20,24},{24,28},{1,5},{5,9},{9,... | collective-permute-start | bytes 46088 | tf_op jit(solution)/shard_map/ppermute | solution.py:20
  62.3 2.1 %collective-permute-start.7 = (f32[5,3,256]{2,1,0:T(4,128)S(1)}, f32[5,3,256]{2,1,0:T(4,128)S(1)}, u32[]{:S(2)}, u32[]{:S(2)}) collective-permute-start(f32[5,3,256]{2,1,0:T(4,128)S(1)} %get-tuple-element.649), channel_id=1, source_target_pairs={{4,0},{8,4},{12,8},{16,12},{20,16},{24,20},{28,24},{5,1},{9,5},{13... | collective-permute-start | bytes 46088 | tf_op jit(solution)/shard_map/ppermute | solution.py:21
  65.5 2.0 %collective-permute-done.7 = f32[5,3,256]{2,1,0:T(4,128)S(1)} collective-permute-done((f32[5,3,256]{2,1,0:T(4,128)S(1)}, f32[5,3,256]{2,1,0:T(4,128)S(1)}, u32[]{:S(2)}, u32[]{:S(2)}) %collective-permute-start.7) | collective-permute-done | bytes 15392 | tf_op jit(solution)/shard_map/ppermute | solution.py:21
  67.8 2.4 %while.76 = (s32[]{:T(128)}, f32[4,5,32]{2,1,0:T(8,128)S(1)}, s32[4,32]{1,0:T(4,128)S(1)}, f32[4,32]{1,0:T(4,128)S(1)}, f32[5,16,256]{2,1,0:T(8,128)S(1)}, /*index=5*/f32[4,32]{1,0:T(4,128)S(1)}, s32[]{:T(128)}) while((s32[]{:T(128)}, f32[4,5,32]{2,1,0:T(8,128)S(1)}, s32[4,32]{1,0:T(4,128)S(1)}, f32[4,32]{1,0:T(4,128)S(1)}, ...), condition=%wide.region_14.15_spmd, body=%wide.region_12.14_spmd.sunk | while | flops 7990722 | bytes 159065 | solution.py:91
  68.0 0.4 fusion.352
  69.2 0.4 fusion.352
  69.8 0.4 fusion.352
  70.2 0.7 all_to_all.52
  70.9 3.9 %all-to-all-start.4 = ((f32[4,1,160]{2,1,0:T(1,128)}), f32[4,1,160]{2,1,0:T(1,128)S(1)}, u32[]{:S(2)}, u32[]{:S(2)}) async-start(f32[4,1,160]{2,1,0:T(1,128)} %all_to_all.52), calls=%async_computation.4 | async-start | bytes 8192 | tf_op jit(solution)/shard_map/all_to_all | solution.py:93
  74.8 2.2 %collective-permute-start.8 = (f32[5,3,256]{2,1,0:T(4,128)S(1)}, f32[5,3,256]{2,1,0:T(4,128)S(1)}, u32[]{:S(2)}, u32[]{:S(2)}) collective-permute-start(f32[5,3,256]{2,1,0:T(4,128)S(1)} %get-tuple-element.640), channel_id=1, source_target_pairs={{0,4},{4,8},{8,12},{12,16},{16,20},{20,24},{24,28},{1,5},{5,9},{9,... | collective-permute-start | bytes 46088 | tf_op jit(solution)/shard_map/ppermute | solution.py:20
  77.0 2.1 %collective-permute-start.9 = (f32[5,3,256]{2,1,0:T(4,128)S(1)}, f32[5,3,256]{2,1,0:T(4,128)S(1)}, u32[]{:S(2)}, u32[]{:S(2)}) collective-permute-start(f32[5,3,256]{2,1,0:T(4,128)S(1)} %get-tuple-element.639), channel_id=1, source_target_pairs={{4,0},{8,4},{12,8},{16,12},{20,16},{24,20},{28,24},{5,1},{9,5},{13... | collective-permute-start | bytes 46088 | tf_op jit(solution)/shard_map/ppermute | solution.py:21
  80.2 2.0 %collective-permute-done.9 = f32[5,3,256]{2,1,0:T(4,128)S(1)} collective-permute-done((f32[5,3,256]{2,1,0:T(4,128)S(1)}, f32[5,3,256]{2,1,0:T(4,128)S(1)}, u32[]{:S(2)}, u32[]{:S(2)}) %collective-permute-start.9) | collective-permute-done | bytes 15392 | tf_op jit(solution)/shard_map/ppermute | solution.py:21
  82.5 2.4 %while.77 = (s32[]{:T(128)}, f32[4,5,32]{2,1,0:T(8,128)S(1)}, s32[4,32]{1,0:T(4,128)S(1)}, f32[4,32]{1,0:T(4,128)S(1)}, f32[5,16,256]{2,1,0:T(8,128)S(1)}, /*index=5*/f32[4,32]{1,0:T(4,128)S(1)}, s32[]{:T(128)}) while((s32[]{:T(128)}, f32[4,5,32]{2,1,0:T(8,128)S(1)}, s32[4,32]{1,0:T(4,128)S(1)}, f32[4,32]{1,0:T(4,128)S(1)}, ...), condition=%wide.region_17.18_spmd, body=%wide.region_15.17_spmd.sunk | while | flops 7990722 | bytes 159065 | solution.py:91
  82.6 0.4 fusion.355
  83.2 0.4 fusion.355
  83.8 0.4 fusion.355
  84.9 0.7 all_to_all.53
  85.5 3.9 %all-to-all-start.5 = ((f32[4,1,160]{2,1,0:T(1,128)}), f32[4,1,160]{2,1,0:T(1,128)S(1)}, u32[]{:S(2)}, u32[]{:S(2)}) async-start(f32[4,1,160]{2,1,0:T(1,128)} %all_to_all.53), calls=%async_computation.5 | async-start | bytes 8192 | tf_op jit(solution)/shard_map/all_to_all | solution.py:93
  89.5 2.2 %collective-permute-start.10 = (f32[5,3,256]{2,1,0:T(4,128)S(1)}, f32[5,3,256]{2,1,0:T(4,128)S(1)}, u32[]{:S(2)}, u32[]{:S(2)}) collective-permute-start(f32[5,3,256]{2,1,0:T(4,128)S(1)} %get-tuple-element.630), channel_id=1, source_target_pairs={{0,4},{4,8},{8,12},{12,16},{16,20},{20,24},{24,28},{1,5},{5,9},{9,... | collective-permute-start | bytes 46088 | tf_op jit(solution)/shard_map/ppermute | solution.py:20
  91.7 2.1 %collective-permute-start.11 = (f32[5,3,256]{2,1,0:T(4,128)S(1)}, f32[5,3,256]{2,1,0:T(4,128)S(1)}, u32[]{:S(2)}, u32[]{:S(2)}) collective-permute-start(f32[5,3,256]{2,1,0:T(4,128)S(1)} %get-tuple-element.629), channel_id=1, source_target_pairs={{4,0},{8,4},{12,8},{16,12},{20,16},{24,20},{28,24},{5,1},{9,5},{13... | collective-permute-start | bytes 46088 | tf_op jit(solution)/shard_map/ppermute | solution.py:21
  94.8 2.0 %collective-permute-done.11 = f32[5,3,256]{2,1,0:T(4,128)S(1)} collective-permute-done((f32[5,3,256]{2,1,0:T(4,128)S(1)}, f32[5,3,256]{2,1,0:T(4,128)S(1)}, u32[]{:S(2)}, u32[]{:S(2)}) %collective-permute-start.11) | collective-permute-done | bytes 15392 | tf_op jit(solution)/shard_map/ppermute | solution.py:21
  96.9 0.8 add_bitcast_fusion
  (268 shorter events, 12.0 us)
Async XLA Ops:
  0.7 0.7 copy-start.1
  8.0 12.3 %all-to-all-start = ((f32[4,1,160]{2,1,0:T(1,128)}), f32[4,1,160]{2,1,0:T(1,128)S(1)}, u32[]{:S(2)}, u32[]{:S(2)}) async-start(f32[4,1,160]{2,1,0:T(1,128)} %all_to_all.48), calls=%async_computation | async-start | bytes 8192 | tf_op jit(solution)/shard_map/all_to_all | solution.py:93
  12.2 7.7 %copy-start.2 = (f32[1,2,16,256]{3,2,1,0:T(8,128)S(1)}, f32[1,2,16,256]{3,2,1,0:T(8,128)}, u32[]{:S(2)}) copy-start(f32[1,2,16,256]{3,2,1,0:T(8,128)} %param.21) | copy-start | bytes 98308
  12.2 7.7 %copy-start.3 = (f32[1,2,16,256]{3,2,1,0:T(8,128)S(1)}, f32[1,2,16,256]{3,2,1,0:T(8,128)}, u32[]{:S(2)}) copy-start(f32[1,2,16,256]{3,2,1,0:T(8,128)} %param.20) | copy-start | bytes 98308
  13.0 6.0 %copy-start.4 = (s32[1,1,4,32]{3,2,1,0:T(4,128)S(1)}, s32[1,1,4,32]{3,2,1,0:T(4,128)}, u32[]{:S(2)}) copy-start(s32[1,1,4,32]{3,2,1,0:T(4,128)} %param.24) | copy-start | bytes 1540
  13.0 8.6 %collective-permute-start = (f32[5,3,256]{2,1,0:T(4,128)S(1)}, f32[5,3,256]{2,1,0:T(4,128)S(1)}, u32[]{:S(2)}, u32[]{:S(2)}) collective-permute-start(f32[5,3,256]{2,1,0:T(4,128)S(1)} %get-tuple-element.680), channel_id=1, source_target_pairs={{0,4},{4,8},{8,12},{12,16},{16,20},{20,24},{24,28},{1,5},{5,9},{9,... | collective-permute-start | bytes 46088 | tf_op jit(solution)/shard_map/ppermute | solution.py:20
  17.1 5.1 %collective-permute-start.1 = (f32[5,3,256]{2,1,0:T(4,128)S(1)}, f32[5,3,256]{2,1,0:T(4,128)S(1)}, u32[]{:S(2)}, u32[]{:S(2)}) collective-permute-start(f32[5,3,256]{2,1,0:T(4,128)S(1)} %get-tuple-element.679), channel_id=1, source_target_pairs={{4,0},{8,4},{12,8},{16,12},{20,16},{24,20},{28,24},{5,1},{9,5},{13... | collective-permute-start | bytes 46088 | tf_op jit(solution)/shard_map/ppermute | solution.py:21
  19.1 0.7 copy-start.5
  20.0 0.9 copy-start
  25.6 9.3 %all-to-all-start.1 = ((f32[4,1,160]{2,1,0:T(1,128)}), f32[4,1,160]{2,1,0:T(1,128)S(1)}, u32[]{:S(2)}, u32[]{:S(2)}) async-start(f32[4,1,160]{2,1,0:T(1,128)} %all_to_all.49), calls=%async_computation.1 | async-start | bytes 8192 | tf_op jit(solution)/shard_map/all_to_all | solution.py:93
  29.6 6.4 %collective-permute-start.2 = (f32[5,3,256]{2,1,0:T(4,128)S(1)}, f32[5,3,256]{2,1,0:T(4,128)S(1)}, u32[]{:S(2)}, u32[]{:S(2)}) collective-permute-start(f32[5,3,256]{2,1,0:T(4,128)S(1)} %get-tuple-element.670), channel_id=1, source_target_pairs={{0,4},{4,8},{8,12},{12,16},{16,20},{20,24},{24,28},{1,5},{5,9},{9,... | collective-permute-start | bytes 46088 | tf_op jit(solution)/shard_map/ppermute | solution.py:20
  33.0 5.1 %collective-permute-start.3 = (f32[5,3,256]{2,1,0:T(4,128)S(1)}, f32[5,3,256]{2,1,0:T(4,128)S(1)}, u32[]{:S(2)}, u32[]{:S(2)}) collective-permute-start(f32[5,3,256]{2,1,0:T(4,128)S(1)} %get-tuple-element.669), channel_id=1, source_target_pairs={{4,0},{8,4},{12,8},{16,12},{20,16},{24,20},{28,24},{5,1},{9,5},{13... | collective-permute-start | bytes 46088 | tf_op jit(solution)/shard_map/ppermute | solution.py:21
  41.5 8.3 %all-to-all-start.2 = ((f32[4,1,160]{2,1,0:T(1,128)}), f32[4,1,160]{2,1,0:T(1,128)S(1)}, u32[]{:S(2)}, u32[]{:S(2)}) async-start(f32[4,1,160]{2,1,0:T(1,128)} %all_to_all.50), calls=%async_computation.2 | async-start | bytes 8192 | tf_op jit(solution)/shard_map/all_to_all | solution.py:93
  45.4 5.4 %collective-permute-start.4 = (f32[5,3,256]{2,1,0:T(4,128)S(1)}, f32[5,3,256]{2,1,0:T(4,128)S(1)}, u32[]{:S(2)}, u32[]{:S(2)}) collective-permute-start(f32[5,3,256]{2,1,0:T(4,128)S(1)} %get-tuple-element.660), channel_id=1, source_target_pairs={{0,4},{4,8},{8,12},{12,16},{16,20},{20,24},{24,28},{1,5},{5,9},{9,... | collective-permute-start | bytes 46088 | tf_op jit(solution)/shard_map/ppermute | solution.py:20
  47.7 5.1 %collective-permute-start.5 = (f32[5,3,256]{2,1,0:T(4,128)S(1)}, f32[5,3,256]{2,1,0:T(4,128)S(1)}, u32[]{:S(2)}, u32[]{:S(2)}) collective-permute-start(f32[5,3,256]{2,1,0:T(4,128)S(1)} %get-tuple-element.659), channel_id=1, source_target_pairs={{4,0},{8,4},{12,8},{16,12},{20,16},{24,20},{28,24},{5,1},{9,5},{13... | collective-permute-start | bytes 46088 | tf_op jit(solution)/shard_map/ppermute | solution.py:21
  56.2 8.3 %all-to-all-start.3 = ((f32[4,1,160]{2,1,0:T(1,128)}), f32[4,1,160]{2,1,0:T(1,128)S(1)}, u32[]{:S(2)}, u32[]{:S(2)}) async-start(f32[4,1,160]{2,1,0:T(1,128)} %all_to_all.51), calls=%async_computation.3 | async-start | bytes 8192 | tf_op jit(solution)/shard_map/all_to_all | solution.py:93
  60.1 5.4 %collective-permute-start.6 = (f32[5,3,256]{2,1,0:T(4,128)S(1)}, f32[5,3,256]{2,1,0:T(4,128)S(1)}, u32[]{:S(2)}, u32[]{:S(2)}) collective-permute-start(f32[5,3,256]{2,1,0:T(4,128)S(1)} %get-tuple-element.650), channel_id=1, source_target_pairs={{0,4},{4,8},{8,12},{12,16},{16,20},{20,24},{24,28},{1,5},{5,9},{9,... | collective-permute-start | bytes 46088 | tf_op jit(solution)/shard_map/ppermute | solution.py:20
  62.3 5.1 %collective-permute-start.7 = (f32[5,3,256]{2,1,0:T(4,128)S(1)}, f32[5,3,256]{2,1,0:T(4,128)S(1)}, u32[]{:S(2)}, u32[]{:S(2)}) collective-permute-start(f32[5,3,256]{2,1,0:T(4,128)S(1)} %get-tuple-element.649), channel_id=1, source_target_pairs={{4,0},{8,4},{12,8},{16,12},{20,16},{24,20},{28,24},{5,1},{9,5},{13... | collective-permute-start | bytes 46088 | tf_op jit(solution)/shard_map/ppermute | solution.py:21
  70.9 8.3 %all-to-all-start.4 = ((f32[4,1,160]{2,1,0:T(1,128)}), f32[4,1,160]{2,1,0:T(1,128)S(1)}, u32[]{:S(2)}, u32[]{:S(2)}) async-start(f32[4,1,160]{2,1,0:T(1,128)} %all_to_all.52), calls=%async_computation.4 | async-start | bytes 8192 | tf_op jit(solution)/shard_map/all_to_all | solution.py:93
  74.8 5.4 %collective-permute-start.8 = (f32[5,3,256]{2,1,0:T(4,128)S(1)}, f32[5,3,256]{2,1,0:T(4,128)S(1)}, u32[]{:S(2)}, u32[]{:S(2)}) collective-permute-start(f32[5,3,256]{2,1,0:T(4,128)S(1)} %get-tuple-element.640), channel_id=1, source_target_pairs={{0,4},{4,8},{8,12},{12,16},{16,20},{20,24},{24,28},{1,5},{5,9},{9,... | collective-permute-start | bytes 46088 | tf_op jit(solution)/shard_map/ppermute | solution.py:20
  77.0 5.1 %collective-permute-start.9 = (f32[5,3,256]{2,1,0:T(4,128)S(1)}, f32[5,3,256]{2,1,0:T(4,128)S(1)}, u32[]{:S(2)}, u32[]{:S(2)}) collective-permute-start(f32[5,3,256]{2,1,0:T(4,128)S(1)} %get-tuple-element.639), channel_id=1, source_target_pairs={{4,0},{8,4},{12,8},{16,12},{20,16},{24,20},{28,24},{5,1},{9,5},{13... | collective-permute-start | bytes 46088 | tf_op jit(solution)/shard_map/ppermute | solution.py:21
  85.5 8.3 %all-to-all-start.5 = ((f32[4,1,160]{2,1,0:T(1,128)}), f32[4,1,160]{2,1,0:T(1,128)S(1)}, u32[]{:S(2)}, u32[]{:S(2)}) async-start(f32[4,1,160]{2,1,0:T(1,128)} %all_to_all.53), calls=%async_computation.5 | async-start | bytes 8192 | tf_op jit(solution)/shard_map/all_to_all | solution.py:93
  89.5 5.4 %collective-permute-start.10 = (f32[5,3,256]{2,1,0:T(4,128)S(1)}, f32[5,3,256]{2,1,0:T(4,128)S(1)}, u32[]{:S(2)}, u32[]{:S(2)}) collective-permute-start(f32[5,3,256]{2,1,0:T(4,128)S(1)} %get-tuple-element.630), channel_id=1, source_target_pairs={{0,4},{4,8},{8,12},{12,16},{16,20},{20,24},{24,28},{1,5},{5,9},{9,... | collective-permute-start | bytes 46088 | tf_op jit(solution)/shard_map/ppermute | solution.py:20
  91.7 5.1 %collective-permute-start.11 = (f32[5,3,256]{2,1,0:T(4,128)S(1)}, f32[5,3,256]{2,1,0:T(4,128)S(1)}, u32[]{:S(2)}, u32[]{:S(2)}) collective-permute-start(f32[5,3,256]{2,1,0:T(4,128)S(1)} %get-tuple-element.629), channel_id=1, source_target_pairs={{4,0},{8,4},{12,8},{16,12},{20,16},{24,20},{28,24},{5,1},{9,5},{13... | collective-permute-start | bytes 46088 | tf_op jit(solution)/shard_map/ppermute | solution.py:21
where the time goes:
time: 98.8 us; the launch traced here: 97.8 us
  starting transfers between devices  52.4 us (53%)
  matrix products  15.3 us (15%)
  local copies, waits for them, and re-layouts  11.2 us (11%)
  waiting for transfers between devices  10.5 us (11%)
  other arithmetic  6.4 us (6%)
  loops' own time  1.21 us (1%)
    all_to_all x6, starting transfers between devices, fringe_local(): lax.all_to_all(outgoing, 'grp', split_axis=0, concat_axis=0, tiled=True)  23.8 us
    ppermute x6, starting transfers between devices, with_halo(): before = lax.ppermute(last, axis, up)  16.3 us
    dot_general x24, matrix products, interpolate(): jnp.einsum('kr,vrc->vkc', row_weight, field, precision=lax.Precision.HIGH...  13.6 us
    ppermute x6, starting transfers between devices, with_halo(): after = lax.ppermute(first, axis, down)  12.3 us
    ppermute x6, waiting for transfers between devices, with_halo(): after = lax.ppermute(first, axis, down)  10.5 us
    all_to_all x6, local copies, waits for them, and re-layouts, fringe_local(): lax.all_to_all(outgoing, 'grp', split_axis=0, concat_axis=0, tiled=True)  4.03 us
    slice x30, local copies, waits for them, and re-layouts, along_y(): return jnp.roll(centre, -offset, axis=-1)  2.38 us
  transfers between devices with their start and end apart: 18, of which 6 were waited for; matrix products, arithmetic and copies ran while one was open for 7% of the time, Pallas kernels for 0%

commit v1 on v0

v1 whole, which is shorter than its diff:
```python
import functools

import jax
import jax.numpy as jnp
from jax import lax
from jax.experimental import pallas as pl
from jax.experimental.pallas import tpu as pltpu
from jax.sharding import PartitionSpec as P

STEPS = 2
TIME_STEP = 0.3
SECTION_COEFS = ((0.0, 1.0), (0.75, 0.25), (1.0 / 3.0, 2.0 / 3.0))
UPWIND = {-3: -2.0, -2: 15.0, -1: -60.0, 0: 20.0, 1: 30.0, 2: -3.0}
SECOND = {-1: 1.0, 0: -2.0, 1: 1.0}
OFFSETS = (-3, -2, -1, 1, 2)
LANES = 128
SUB = 8
MESH = pl.DeviceIdType.MESH


def split_bf16(x):
    hi = x.astype(jnp.bfloat16)
    lo = (x - hi.astype(jnp.float32)).astype(jnp.bfloat16)
    return hi, lo


def kernel(
    state_hbm,
    adv_hbm,
    visc_hbm,
    cell_hbm,
    frac_hbm,
    fringe_hbm,
    count_ref,
    out_hbm,
    sbuf,
    start_buf,
    pad,
    adv,
    visc,
    cells,
    fracs,
    fringes,
    wide,
    coef,
    pick_mat,
    pick_w,
    place_mat,
    place_rows,
    hit,
    val,
    recv,
    local_sem,
    face_send,
    face_recv,
    slot_send,
    slot_recv,
):
    nvar, rows, halves = sbuf.shape[2], sbuf.shape[3], sbuf.shape[1]
    cols = halves * LANES
    groups, slots = cells.shape
    total = groups * slots
    tiles = total // LANES
    per_tile = LANES // slots
    blk = lax.axis_index("blk")
    grp = lax.axis_index("grp")
    nblk = lax.axis_size("blk")
    has_up = blk > 0
    has_down = blk < nblk - 1
    row_tiles = rows // SUB

    copies = []

    def fetch(src, dst):
        copy = pltpu.make_async_copy(src, dst, local_sem.at[len(copies)])
        copy.start()
        copies.append(copy)
        return copy

    state_copies = [
        fetch(state_hbm.at[0, :, :, pl.ds(h * LANES, LANES)], sbuf.at[0, h]) for h in range(halves)
    ]
    donor_copies = [fetch(cell_hbm.at[0, 0], cells), fetch(frac_hbm.at[0, 0], fracs)]
    fringe_copies = [fetch(fringe_hbm.at[0, 0], fringes)]
    coef_copies = [fetch(adv_hbm.at[0], adv), fetch(visc_hbm.at[0], visc)]

    zero_face = jnp.zeros((halves, nvar, SUB, LANES), jnp.float32)
    for slot in range(2):
        pad[slot, :, :, 0:SUB, :] = zero_face
        pad[slot, :, :, SUB + rows : 2 * SUB + rows, :] = zero_face

    barrier = pltpu.get_barrier_semaphore()
    for j in range(1, groups):
        pl.semaphore_signal(
            barrier, inc=1, device_id=(blk, lax.rem(grp + j, groups)), device_id_type=MESH
        )

    @pl.when(has_up)
    def _():
        pl.semaphore_signal(barrier, inc=1, device_id=(blk - 1, grp), device_id_type=MESH)

    @pl.when(has_down)
    def _():
        pl.semaphore_signal(barrier, inc=1, device_id=(blk + 1, grp), device_id_type=MESH)

    wide[...] = jnp.zeros_like(wide)
    for copy in donor_copies:
        copy.wait()

    lane_block = lax.broadcasted_iota(jnp.int32, (groups, LANES), 1) // slots
    row_id = lax.broadcasted_iota(jnp.int32, (groups, LANES), 0)

    def to_lanes(index, value, sign):
        wide[index, :, 0:slots] = value
        full = wide[index]
        spread = full
        for b in range(1, per_tile):
            spread = jnp.where(lane_block == b, pltpu.roll(full, slots * b, 1), spread)
        pieces = []
        for t in range(tiles):
            source = lax.rem(grp + sign * (t * per_tile + lane_block) + groups, groups)
            pieces.append(
                jnp.sum(jnp.where(row_id == source, spread, 0.0), axis=0, keepdims=True)
            )
        return pieces[0] if tiles == 1 else jnp.concatenate(pieces, axis=1)

    def row_and_col(cell):
        if cols & (cols - 1) == 0:
            return lax.shift_right_logical(cell, cols.bit_length() - 1), cell & (cols - 1)
        return cell // cols, cell % cols

    corner = to_lanes(0, cells[...].astype(jnp.float32), 1).astype(jnp.int32)
    frac_x = to_lanes(1, fracs[0], 1)
    frac_y = to_lanes(2, fracs[1], 1)
    corner_row, corner_col = row_and_col(corner)
    next_col = jnp.where(corner_col == cols - 1, 0, corner_col + 1)
    col_iota = lax.broadcasted_iota(jnp.int32, (cols, total), 0)
    row_iota = lax.broadcasted_iota(jnp.int32, (rows, total), 0)

    def one_hot(iota, index):
        return jnp.where(iota == index, 1.0, 0.0)

    pick_mat[:, 0:total] = one_hot(col_iota, corner_col).astype(jnp.bfloat16)
    pick_mat[:, total : 2 * total] = one_hot(col_iota, next_col).astype(jnp.bfloat16)
    row_weight = (1.0 - frac_x) * one_hot(row_iota, corner_row) + frac_x * one_hot(
        row_iota, corner_row + 1
    )
    pick_w[0] = (1.0 - frac_y) * row_weight
    pick_w[1] = frac_y * row_weight

    for copy in state_copies:
        copy.wait()
    for h in range(halves):
        start_buf[h] = sbuf[0, h]

    pl.semaphore_wait(barrier, groups - 1 + has_up.astype(jnp.int32) + has_down.astype(jnp.int32))

    def face_copy(slot, way):
        first = 0 if way == 0 else rows - SUB
        landing = SUB + rows if way == 0 else 0
        return pltpu.make_async_remote_copy(
            src_ref=sbuf.at[slot, :, :, pl.ds(first, SUB), :],
            dst_ref=pad.at[slot, :, :, pl.ds(landing, SUB), :],
            send_sem=face_send.at[slot, way],
            recv_sem=face_recv.at[slot, way],
            device_id=((blk - 1) if way == 0 else (blk + 1), grp),
            device_id_type=MESH,
        )

    def slot_copy(slot, j):
        return pltpu.make_async_remote_copy(
            src_ref=val.at[slot, :, pl.ds((j // per_tile) * LANES, LANES)],
            dst_ref=recv.at[slot, j],
            send_sem=slot_send.at[slot, j],
            recv_sem=slot_recv.at[slot, j],
            device_id=(blk, lax.rem(grp + j, groups)),
            device_id_type=MESH,
        )

    def send_faces(slot):
        @pl.when(has_up)
        def _():
            face_copy(slot, 0).start()

        @pl.when(has_down)
        def _():
            face_copy(slot, 1).start()

    def send_slots(slot):
        s = [sbuf[slot, h].reshape(nvar * rows, LANES) for h in range(halves)]
        whole = s[0] if halves == 1 else jnp.concatenate(s, axis=1)
        hi, lo = split_bf16(whole)
        mat = pick_mat[...]
        got = jnp.dot(hi, mat, preferred_element_type=jnp.float32) + jnp.dot(
            lo, mat, preferred_element_type=jnp.float32
        )
        here = got[:, 0:total].reshape(nvar, rows, total)
        there = got[:, total : 2 * total].reshape(nvar, rows, total)
        val[slot] = jnp.sum(here * pick_w[0][None] + there * pick_w[1][None], axis=1)
        for j in range(groups - 1, 0, -1):
            slot_copy(slot, j).start()

    def prepare():
        for copy in fringe_copies:
            copy.wait()
        target = to_lanes(3, fringes[...].astype(jnp.float32), -1).astype(jnp.int32)
        lane_id = lax.broadcasted_iota(jnp.int32, (1, total), 1)
        lane_slot = lax.rem(lane_id, slots)
        live = jnp.zeros((1, total), jnp.int32)
        for j in range(groups):
            source = lax.rem(grp - j + groups, groups)
            live = jnp.where(lane_id // slots == j, count_ref[0, 0, source], live)
        target_row, target_col = row_and_col(target)
        target_rows = jnp.where((row_iota == target_row) & (lane_slot < live), 1.0, 0.0)
        place_rows[...] = target_rows
        target_cols = one_hot(col_iota, target_col)
        by_slot = jnp.transpose(target_cols).astype(jnp.bfloat16)
        place_mat[0:total, :] = by_slot
        place_mat[total : 2 * total, :] = by_slot
        hit[...] = jnp.dot(
            target_rows.astype(jnp.bfloat16), by_slot, preferred_element_type=jnp.float32
        )
        for copy in coef_copies:
            copy.wait()
        for h in range(halves):
            window = slice(h * LANES, (h + 1) * LANES)
            centre = 1.0
            for d in range(2):
                speed = adv[d, :, window] * (-TIME_STEP / 60.0)
                visco = visc[d, :, window] * TIME_STEP
                for n, o in enumerate(OFFSETS):
                    c = speed * UPWIND[o]
                    if o in SECOND:
                        c = c + visco * SECOND[o]
                    coef[d * len(OFFSETS) + n, h] = c
                centre = centre + speed * UPWIND[0] + visco * SECOND[0]
            coef[2 * len(OFFSETS), h] = centre

    def receive_slots(slot):
        lane = lax.broadcasted_iota(jnp.int32, (nvar, LANES), 1) // slots
        pieces = []
        for t in range(tiles):
            piece = val[slot, :, t * LANES : (t + 1) * LANES]
            for b in range(per_tile):
                j = t * per_tile + b
                if j > 0:
                    slot_copy(slot, j).wait_recv()
                    piece = jnp.where(lane == b, recv[slot, j], piece)
            pieces.append(piece)
        return pieces[0] if tiles == 1 else jnp.concatenate(pieces, axis=1)

    def fill(slot):
        incoming = receive_slots(slot)
        spread = (incoming[:, None, :] * place_rows[...][None]).reshape(nvar * rows, total)
        hi, lo = split_bf16(spread)
        placed = jnp.dot(
            jnp.concatenate([hi, lo], axis=1), place_mat[...], preferred_element_type=jnp.float32
        )
        for h in range(halves):
            window = slice(h * LANES, (h + 1) * LANES)
            hit_h = hit[:, window] > 0.5
            for f in range(nvar):
                pad[slot, h, f, SUB : SUB + rows, :] = jnp.where(
                    hit_h, placed[f * rows : (f + 1) * rows, window], sbuf[slot, h, f]
                )

    lane = lax.broadcasted_iota(jnp.int32, (SUB, LANES), 1)

    def along_y(centre, o):
        rolled = [pltpu.roll(c, (-o) % LANES, 1) for c in centre]
        if o > 0:
            mask = lane < LANES - o
            return [
                jnp.where(mask, rolled[h], rolled[(h + 1) % halves]) for h in range(halves)
            ]
        mask = lane >= -o
        return [jnp.where(mask, rolled[h], rolled[(h - 1) % halves]) for h in range(halves)]

    def advance(slot, old, new, store):
        count = len(OFFSETS)
        for i in range(row_tiles):
            base = SUB + i * SUB
            grads = {}
            results = {}
            for f in range(nvar):
                centre = [pad[slot, h, f, base : base + SUB, :] for h in range(halves)]
                total_f = [
                    coef[2 * count, h, i * SUB : (i + 1) * SUB, :] * centre[h]
                    for h in range(halves)
                ]
                xs, ys = {}, {}
                for n, o in enumerate(OFFSETS):
                    xs[o] = [
                        pad[slot, h, f, base + o : base + o + SUB, :] for h in range(halves)
                    ]
                    ys[o] = along_y(centre, o)
                    for h in range(halves):
                        rows_i = slice(i * SUB, (i + 1) * SUB)
                        total_f[h] = (
                            total_f[h]
                            + coef[n, h, rows_i, :] * xs[o][h]
                            + coef[count + n, h, rows_i, :] * ys[o][h]
                        )

                def central(vals):
                    return [
                        (vals[-2][h] - vals[2][h]) + 8.0 * (vals[1][h] - vals[-1][h])
                        for h in range(halves)
                    ]

                if f in (1, 4):
                    grads[f, 0] = central(xs)
                if f in (2, 4):
                    grads[f, 1] = central(ys)
                results[f] = total_f
            for h in range(halves):
                scale = TIME_STEP / 12.0
                diverge = (grads[1, 0][h] + grads[2, 1][h]) * scale
                results[0][h] = results[0][h] - diverge
                results[4][h] = results[4][h] - diverge
                results[1][h] = results[1][h] - grads[4, 0][h] * scale
                results[2][h] = results[2][h] - grads[4, 1][h] * scale
                for f in range(nvar):
                    rows_i = slice(i * SUB, (i + 1) * SUB)
                    value = results[f][h]
                    if new != 1.0:
                        value = new * value
                    if old != 0.0:
                        value = value + old * start_buf[h, f, rows_i, :]
                    store(h, f, rows_i, value)

    sections = [c for _ in range(STEPS) for c in SECTION_COEFS]
    for n, (old, new) in enumerate(sections):
        slot = n % 2
        last = n == len(sections) - 1
        step_end = (n + 1) % len(SECTION_COEFS) == 0
        send_faces(slot)
        send_slots(slot)
        if n == 0:
            prepare()
        fill(slot)

        @pl.when(has_up)
        def _():
            face_copy(slot, 1).wait_recv()

        @pl.when(has_down)
        def _():
            face_copy(slot, 0).wait_recv()

        def store(h, f, rows_i, value):
            sbuf[1 - slot, h, f, rows_i, :] = value

        advance(slot, old, new, store)
        if step_end and not last:
            for h in range(halves):
                start_buf[h] = sbuf[1 - slot, h]

        @pl.when(has_up)
        def _():
            face_copy(slot, 0).wait_send()

        @pl.when(has_down)
        def _():
            face_copy(slot, 1).wait_send()

        for j in range(1, groups):
            slot_copy(slot, j).wait_send()

    final = len(sections) % 2
    writes = [
        pltpu.make_async_copy(
            sbuf.at[final, h], out_hbm.at[0, :, :, pl.ds(h * LANES, LANES)], local_sem.at[h]
        )
        for h in range(halves)
    ]
    for copy in writes:
        copy.start()
    for copy in writes:
        copy.wait()


def body(state, advection, viscosity, donor_cell, donor_frac, fringe_cell, fringe_count):
    _, nvar, rows, cols = state.shape
    groups, slots = donor_cell.shape[2:]
    total = groups * slots
    halves = cols // LANES
    f32 = jnp.float32
    hbm = pl.BlockSpec(memory_space=pl.ANY)
    return pl.pallas_call(
        kernel,
        out_shape=jax.ShapeDtypeStruct(state.shape, f32),
        in_specs=[hbm] * 6 + [pl.BlockSpec(memory_space=pltpu.SMEM)],
        out_specs=hbm,
        scratch_shapes=[
            pltpu.VMEM((2, halves, nvar, rows, LANES), f32),
            pltpu.VMEM((halves, nvar, rows, LANES), f32),
            pltpu.VMEM((2, halves, nvar, rows + 2 * SUB, LANES), f32),
            pltpu.VMEM((2, rows, cols), f32),
            pltpu.VMEM((2, rows, cols), f32),
            pltpu.VMEM((groups, slots), jnp.int32),
            pltpu.VMEM((2, groups, slots), f32),
            pltpu.VMEM((groups, slots), jnp.int32),
            pltpu.VMEM((4, groups, LANES), f32),
            pltpu.VMEM((2 * len(OFFSETS) + 1, halves, rows, LANES), f32),
            pltpu.VMEM((cols, 2 * total), jnp.bfloat16),
            pltpu.VMEM((2, rows, total), f32),
            pltpu.VMEM((2 * total, cols), jnp.bfloat16),
            pltpu.VMEM((rows, total), f32),
            pltpu.VMEM((rows, cols), f32),
            pltpu.VMEM((2, nvar, total), f32),
            pltpu.VMEM((2, groups, nvar, LANES), f32),
            pltpu.SemaphoreType.DMA((halves + 5,)),
            pltpu.SemaphoreType.DMA((2, 2)),
            pltpu.SemaphoreType.DMA((2, 2)),
            pltpu.SemaphoreType.DMA((2, groups)),
            pltpu.SemaphoreType.DMA((2, groups)),
        ],
        compiler_params=pltpu.CompilerParams(collective_id=0, has_side_effects=True),
        name="overset_steps",
    )(state, advection, viscosity, donor_cell, donor_frac, fringe_cell, fringe_count)


def solution(mesh):
    placed = (
        P("grp", None, "blk", None),
        P("grp", None, "blk", None),
        P("grp", None, "blk", None),
        P("blk", "grp", None, None),
        P("blk", "grp", None, None, None),
        P("blk", "grp", None, None),
        P("blk", "grp", None),
    )
    return jax.shard_map(
        body, mesh=mesh, in_specs=placed, out_specs=P("grp", None, "blk", None), check_vma=False
    )
```

time: 98.8 us -> 29 us (0.29)
  the two profiles are of different devices: /device:TPU:1 before, /device:TPU:0 now
where the time goes in v1:
time: 29 us; the launch traced here: 28.8 us
  Pallas kernels  27.3 us (94%)
  local copies, waits for them, and re-layouts  1.53 us (5%)
    pallas_call x1, Pallas kernels, body(): pl.pallas_call(kernel, out_shape=jax.ShapeDtypeStruct(state.shape, f32),...  27.3 us
    unnamed x1, local copies, waits for them, and re-layouts  1.53 us

profile of v1, /device:TPU:0, one launch (start us, length us, event | category | flops | bytes accessed | tf_op | source)
XLA Modules:
  0.0 28.8 jit_solution(18234379508796852421)
XLA Ops:
  0.0 27.3 %overset_steps.1 = f32[1,5,16,256]{3,2,1,0:T(8,128)} custom-call(f32[1,5,16,256]{3,2,1,0:T(8,128)} %state_hbm.1, f32[1,2,16,256]{3,2,1,0:T(8,128)} %adv_hbm.1, f32[1,2,16,256]{3,2,1,0:T(8,128)} %visc_hbm.1, s32[1,1,4,32]{3,2,1,0:T(4,128)} %cell_hbm.1, f32[1,1,2,4,32]{4,3,2,1,0:T(4,128)} %frac_hbm.1, s32[1,1,4,32]{3,2,1,0:T(4,128)} %fringe_hbm.1, ...), custom_call_target="tpu_custom_call" | custom-call | tf_op jit(solution)/shard_map/overset_steps/pallas_call | solution.py:390
  27.3 1.5 %copy.9 = f32[1,5,16,256]{3,2,1,0:T(8,128)} copy(f32[1,5,16,256]{3,2,1,0:T(8,128)} %overset_steps.1) | data formatting | bytes 163840
